TPU v7x, 32 devices: a whole 2x2x4 slice. The times are simulated.
32 devices in a mesh: rows: 8 (over z, x), cols: 4 (over y, core).
Axes of the slice: x: 2, y: 2, z: 4, core: 2. Of those that a mesh axis runs over, the one named last changes fastest.
Arguments:
- cube: float32 [1, 12288, 12288], P(None, 'rows', 'cols'), may hold values from -480 to 480
Outputs:
- scale_one: float32 [1, 12288, 12288], P(None, 'rows', 'cols')
- scale_two: float32 [1, 12288, 12288], P(None, 'rows', 'cols')
- scale_three: float32 [1, 12288, 12288], P(None, 'rows', 'cols')
- smooth: float32 [1, 12288, 12288], P(None, 'rows', 'cols')
- sigmas: float32 [3, 1], replicated
All inputs are finite; a program needn't handle non-finite values.
Results may differ from a plain program's by a relative error of at most 0.0002.
Values sent between devices are 32-bit elements; how exact they have to be, the bound alone decides.
No kernel may reach another device: no remote copies, remote signals or barrier semaphores. Data moves between devices by JAX's collectives and lax.ppermute only.
A program may use at most 192 MiB of HBM per device.

v0:
```python
import jax
import jax.numpy as jnp
from jax import lax
from jax.sharding import PartitionSpec as P

LEVELS = 3


def padded_2(array, sides, width):
    for axis, dim in sides:
        count, length = (lax.axis_size(axis), array.shape[dim])
        up = [(i, (i + 1) % count) for i in range(count - 1)]
        down = [(j, i) for i, j in up]
        last = lax.slice_in_dim(array, length - width, length, axis=dim)
        leading = lax.slice_in_dim(array, 0, width, axis=dim)
        before = lax.ppermute(last, axis, up)
        after = lax.ppermute(leading, axis, down)
        array = jnp.concatenate([before, array, after], axis=dim)
    return array


def filter_dim(x, dim, step):
    length = x.shape[dim]

    def part(lower, upper):
        return lax.slice_in_dim(x, lower, length - upper, axis=dim)

    outer = (part(0, 4 * step) + part(4 * step, 0)) * 0.0625
    inner = (part(step, 3 * step) + part(3 * step, step)) * 0.25
    return outer + inner + part(2 * step, 2 * step) * 0.375


def mirror_edges(padded, dim, width, position, extent):
    length = padded.shape[dim]
    upper_mirror = jnp.flip(lax.slice_in_dim(padded, width + 1, 2 * width + 1, axis=dim), dim)
    lower_mirror = jnp.flip(
        lax.slice_in_dim(padded, length - 2 * width - 1, length - width - 1, axis=dim), dim
    )
    upper_rim = lax.slice_in_dim(padded, 0, width, axis=dim)
    lower_rim = lax.slice_in_dim(padded, length - width, length, axis=dim)
    middle = lax.slice_in_dim(padded, width, length - width, axis=dim)
    upper_rim = jnp.where(position == 0, upper_mirror, upper_rim)
    lower_rim = jnp.where(position == extent - 1, lower_mirror, lower_rim)
    return jnp.concatenate([upper_rim, middle, lower_rim], axis=dim)


def on_device(cube):
    row_pos = lax.axis_index("rows")
    col_pos = lax.axis_index("cols")
    row_count = lax.axis_size("rows")
    col_count = lax.axis_size("cols")
    pixels = float(row_count * col_count * cube.shape[1] * cube.shape[2])
    planes = []
    sigma_rows = []

    def record(plane):
        square = jnp.sum(plane * plane, axis=(1, 2))
        square = lax.psum(square, ("rows", "cols"))
        sigma_rows.append(jnp.sqrt(square / pixels + 1e-06))

    current = cube
    for level in range(LEVELS):
        step = 2**level
        width = 2 * step
        tall = padded_2(current, (("rows", 1),), width)
        tall = mirror_edges(tall, 1, width, row_pos, row_count)
        filtered = filter_dim(tall, 1, step)
        broad = padded_2(filtered, (("cols", 2),), width)
        broad = mirror_edges(broad, 2, width, col_pos, col_count)
        nextsmooth = filter_dim(broad, 2, step)
        plane = current - nextsmooth
        planes.append(plane)
        record(plane)
        current = nextsmooth
    sigmas = jnp.stack(sigma_rows)
    return (planes[0], planes[1], planes[2], current, sigmas)


def solution(mesh):
    in_specs = (P(None, "rows", "cols"),)
    out_specs = (
        P(None, "rows", "cols"),
        P(None, "rows", "cols"),
        P(None, "rows", "cols"),
        P(None, "rows", "cols"),
        P(),
    )
    return jax.shard_map(
        on_device, mesh=mesh, in_specs=in_specs, out_specs=out_specs, check_vma=False
    )
```

profile of v0, /device:TPU:0, one launch (start us, length us, event | category | flops | bytes accessed | tf_op | source)
XLA Modules:
  0.0 546.7 jit_solution(906147334425397631)
XLA Ops:
  3.0 5.5 %collective-permute-start = (f32[1,2,3072]{2,1,0:T(2,128)S(1)}, f32[1,2,3072]{2,1,0:T(2,128)S(1)}, u32[]{:S(2)}, u32[]{:S(2)}) collective-permute-start(f32[1,2,3072]{2,1,0:T(2,128)S(1)} %get-tuple-element.47), channel_id=1, source_target_pairs={{0,4},{4,8},{8,12},{12,16},{16,20},{20,24},{24,28},{1,5},{5,9},{9,... | collective-permute-start | bytes 73736 | tf_op jit(solution)/shard_map/ppermute | solution.py:16
  8.5 18.6 %copy.23 = f32[1,1536,3072]{1,2,0:T(8,128)} copy(f32[1,1536,3072]{2,1,0:T(8,128)} %param.1) | data formatting | bytes 37748736 | tf_op args[0]
  29.5 50.3 %fusion.34 = f32[1,1536,3072]{1,2,0:T(8,128)} fusion(f32[1,1536,3072]{1,2,0:T(8,128)} %copy.23, f32[1,2,3072]{1,2,0:T(8,128)S(1)} %copy.21, f32[1,2,3072]{1,2,0:T(8,128)S(1)} %copy.18), kind=kLoop, calls=%fused_computation.58 | loop fusion | flops 51904512 | bytes 37797888 | tf_op jit(solution)/shard_map/add | solution.py:30
  84.1 3.9 collective-permute-done.3
  88.0 50.7 %multiply_reduce_fusion.2 = (f32[]{:T(128)}, f32[1,1536,3072]{1,2,0:T(8,128)}, f32[1,1536,3072]{1,2,0:T(8,128)}) fusion(f32[1,1536,3072]{1,2,0:T(8,128)} %copy.23, f32[1,1536,3072]{1,2,0:T(8,128)} %fusion.34, f32[1,1536,2]{1,2,0:T(2,128)S(1)} %broadcast_select_fusion.10, f32[1,1536,2]{1,2,0:T(2,128)S(1)} %broadcast_select_fusion.11), kind=kLoop, calls=%fused_computation.86 | loop fusion | flops 66060288 | bytes 75522048 | tf_op jit(solution)/shard_map/reduce_sum | solution.py:57
  138.7 6.1 %fusion.54 = (f32[1,4,3072]{1,2,0:T(8,128)}, f32[1,4,3072]{1,2,0:T(8,128)}, f32[1,4,3072]{1,2,0:T(8,128)S(1)}, f32[1,4,3072]{1,2,0:T(8,128)S(1)}) fusion(f32[1,1536,3072]{1,2,0:T(8,128)} %get-tuple-element.20), kind=kLoop, calls=%fused_computation.103 | loop fusion | bytes 393216 | tf_op jit(solution)/shard_map/slice | solution.py:14
  144.8 1.9 copy.26
  147.9 1.9 copy.24
  149.8 5.1 collective-permute-start.4
  154.9 8.7 %rev.47 = f32[1,4,3072]{1,2,0:T(8,128)} reverse(f32[1,4,3072]{1,2,0:T(8,128)S(1)} %get-tuple-element.41), dimensions={1} | reverse | bytes 98304 | tf_op jit(solution)/shard_map/jit(_flip)/rev | solution.py:36
  163.6 2.1 rev.46
  165.8 1.7 copy.27
  169.0 1.7 copy.25
  170.8 50.7 %fusion.28 = f32[1,1536,3072]{1,2,0:T(8,128)} fusion(f32[1,1536,3072]{1,2,0:T(8,128)} %get-tuple-element.20, f32[1,4,3072]{1,2,0:T(8,128)S(1)} %broadcast_select_fusion.2, f32[1,4,3072]{1,2,0:T(8,128)S(1)} %broadcast_select_fusion.3), kind=kLoop, calls=%fused_computation.52 | loop fusion | flops 51904512 | bytes 37847040 | tf_op jit(solution)/shard_map/add | solution.py:30
  222.5 4.1 collective-permute-start.6
  228.5 1.8 collective-permute-done.7
  230.3 50.8 %multiply_reduce_fusion.1 = (f32[]{:T(128)}, f32[1,1536,3072]{1,2,0:T(8,128)}, f32[1,1536,3072]{1,2,0:T(8,128)}) fusion(f32[1,1536,3072]{1,2,0:T(8,128)} %get-tuple-element.20, f32[1,1536,3072]{1,2,0:T(8,128)} %fusion.28, f32[1,1536,4]{1,2,0:T(4,128)S(1)} %broadcast_select_fusion.8, f32[1,1536,4]{1,2,0:T(4,128)S(1)} %broadcast_select_fusion.9), kind=kLoop, calls=%fused_computation.85 | loop fusion | flops 66060288 | bytes 75546624 | tf_op jit(solution)/shard_map/reduce_sum | solution.py:57
  281.1 6.0 %fusion.52 = (f32[1,8,3072]{1,2,0:T(8,128)}, f32[1,8,3072]{1,2,0:T(8,128)}, f32[1,8,3072]{1,2,0:T(8,128)S(1)}, f32[1,8,3072]{1,2,0:T(8,128)S(1)}) fusion(f32[1,1536,3072]{1,2,0:T(8,128)} %get-tuple-element.23), kind=kLoop, calls=%fused_computation.101 | loop fusion | bytes 786432 | tf_op jit(solution)/shard_map/slice | solution.py:14
  287.2 1.8 copy.30
  290.3 1.8 copy.28
  292.2 6.9 %collective-permute-start.8 = (f32[1,8,3072]{2,1,0:T(8,128)S(1)}, f32[1,8,3072]{2,1,0:T(8,128)S(1)}, u32[]{:S(2)}, u32[]{:S(2)}) collective-permute-start(f32[1,8,3072]{2,1,0:T(8,128)S(1)} %copy.28), channel_id=1, source_target_pairs={{0,4},{4,8},{8,12},{12,16},{16,20},{20,24},{24,28},{1,5},{5,9},{9,... | collective-permute-start | bytes 294920 | tf_op jit(solution)/shard_map/ppermute | solution.py:16
  299.0 8.7 %rev.51 = f32[1,8,3072]{1,2,0:T(8,128)} reverse(f32[1,8,3072]{1,2,0:T(8,128)S(1)} %get-tuple-element.33), dimensions={1} | reverse | bytes 196608 | tf_op jit(solution)/shard_map/jit(_flip)/rev | solution.py:36
  307.8 2.1 rev.50
  314.9 51.1 %fusion.22 = f32[1,1536,3072]{1,2,0:T(8,128)} fusion(f32[1,1536,3072]{1,2,0:T(8,128)} %get-tuple-element.23, f32[1,8,3072]{1,2,0:T(8,128)S(1)} %broadcast_select_fusion, f32[1,8,3072]{1,2,0:T(8,128)S(1)} %broadcast_select_fusion.1), kind=kLoop, calls=%fused_computation.46 | loop fusion | flops 51904512 | bytes 37945344 | tf_op jit(solution)/shard_map/add | solution.py:30
  367.0 4.2 collective-permute-start.10
  371.2 18.6 %copy.32 = f32[1,1536,3072]{2,1,0:T(8,128)} copy(f32[1,1536,3072]{1,2,0:T(8,128)} %get-tuple-element.19) | data formatting | bytes 37748736
  389.8 18.6 %copy.33 = f32[1,1536,3072]{2,1,0:T(8,128)} copy(f32[1,1536,3072]{1,2,0:T(8,128)} %get-tuple-element.22) | data formatting | bytes 37748736
  410.2 1.8 collective-permute-done.11
  412.0 50.3 %multiply_reduce_fusion = (f32[]{:T(128)}, f32[1,1536,3072]{1,2,0:T(8,128)}, f32[1,1536,3072]{1,2,0:T(8,128)}) fusion(f32[1,1536,3072]{1,2,0:T(8,128)} %get-tuple-element.23, f32[1,1536,3072]{1,2,0:T(8,128)} %fusion.22, f32[1,1536,8]{1,2,0:T(8,128)S(1)} %broadcast_select_fusion.4, f32[1,1536,8]{1,2,0:T(8,128)S(1)} %broadcast_select_fusion.5), kind=kLoop, calls=%fused_computation.84 | loop fusion | flops 66060288 | bytes 75595776 | tf_op jit(solution)/shard_map/reduce_sum | solution.py:57
  462.2 18.6 %copy.34 = f32[1,1536,3072]{2,1,0:T(8,128)} copy(f32[1,1536,3072]{1,2,0:T(8,128)} %get-tuple-element.25) | data formatting | bytes 37748736
  480.9 44.6 %all-reduce = (f32[1]{0:T(128)}, f32[1]{0:T(128)}, f32[1]{0:T(128)}) all-reduce(f32[1]{0:T(128)} %bitcast.4, f32[1]{0:T(128)} %bitcast.2, f32[1]{0:T(128)} %bitcast), channel_id=1, replica_groups=mesh['rows'=8,'cols'=4] {'rows','cols'}, use_global_device_ids=true, to_apply=%region_5.6 | all-reduce | flops 3 | bytes 24 | tf_op jit(solution)/shard_map/psum | solution.py:58
  527.5 18.6 %copy.35 = f32[1,1536,3072]{2,1,0:T(8,128)} copy(f32[1,1536,3072]{1,2,0:T(8,128)} %get-tuple-element.26) | data formatting | bytes 37748736
  (45 shorter events, 24.4 us)
Async XLA Ops:
  1.7 26.6 %collective-permute-start.1 = (f32[1,2,3072]{2,1,0:T(2,128)S(1)}, f32[1,2,3072]{2,1,0:T(2,128)S(1)}, u32[]{:S(2)}, u32[]{:S(2)}) collective-permute-start(f32[1,2,3072]{2,1,0:T(2,128)S(1)} %get-tuple-element.48), channel_id=1, source_target_pairs={{4,0},{8,4},{12,8},{16,12},{20,16},{24,20},{28,24},{5,1},{9,5},{13... | collective-permute-start | bytes 73736 | tf_op jit(solution)/shard_map/ppermute | solution.py:17
  3.0 25.9 %collective-permute-start = (f32[1,2,3072]{2,1,0:T(2,128)S(1)}, f32[1,2,3072]{2,1,0:T(2,128)S(1)}, u32[]{:S(2)}, u32[]{:S(2)}) collective-permute-start(f32[1,2,3072]{2,1,0:T(2,128)S(1)} %get-tuple-element.47), channel_id=1, source_target_pairs={{0,4},{4,8},{8,12},{12,16},{16,20},{20,24},{24,28},{1,5},{5,9},{9,... | collective-permute-start | bytes 73736 | tf_op jit(solution)/shard_map/ppermute | solution.py:16
  80.7 3.4 collective-permute-start.2
  82.8 5.2 collective-permute-start.3
  146.6 19.1 %collective-permute-start.5 = (f32[1,4,3072]{2,1,0:T(4,128)S(1)}, f32[1,4,3072]{2,1,0:T(4,128)S(1)}, u32[]{:S(2)}, u32[]{:S(2)}) collective-permute-start(f32[1,4,3072]{2,1,0:T(4,128)S(1)} %copy.26), channel_id=1, source_target_pairs={{4,0},{8,4},{12,8},{16,12},{20,16},{24,20},{28,24},{5,1},{9,5},{13... | collective-permute-start | bytes 147464 | tf_op jit(solution)/shard_map/ppermute | solution.py:17
  149.8 19.2 %collective-permute-start.4 = (f32[1,4,3072]{2,1,0:T(4,128)S(1)}, f32[1,4,3072]{2,1,0:T(4,128)S(1)}, u32[]{:S(2)}, u32[]{:S(2)}) collective-permute-start(f32[1,4,3072]{2,1,0:T(4,128)S(1)} %copy.24), channel_id=1, source_target_pairs={{0,4},{4,8},{8,12},{12,16},{16,20},{20,24},{24,28},{1,5},{5,9},{9,... | collective-permute-start | bytes 147464 | tf_op jit(solution)/shard_map/ppermute | solution.py:16
  222.5 6.0 %collective-permute-start.6 = (f32[1,1536,4]{1,2,0:T(4,128)S(1)}, f32[1,1536,4]{1,2,0:T(4,128)S(1)}, u32[]{:S(2)}, u32[]{:S(2)}) collective-permute-start(f32[1,1536,4]{1,2,0:T(4,128)S(1)} %get-tuple-element.35), channel_id=1, source_target_pairs={{0,1},{1,2},{2,3},{4,5},{5,6},{6,7},{8,9},{9,10},{10,11},{12,13},{... | collective-permute-start | bytes 73736 | tf_op jit(solution)/shard_map/ppermute | solution.py:16
  227.2 3.1 collective-permute-start.7
  289.0 20.9 %collective-permute-start.9 = (f32[1,8,3072]{2,1,0:T(8,128)S(1)}, f32[1,8,3072]{2,1,0:T(8,128)S(1)}, u32[]{:S(2)}, u32[]{:S(2)}) collective-permute-start(f32[1,8,3072]{2,1,0:T(8,128)S(1)} %copy.30), channel_id=1, source_target_pairs={{4,0},{8,4},{12,8},{16,12},{20,16},{24,20},{28,24},{5,1},{9,5},{13... | collective-permute-start | bytes 294920 | tf_op jit(solution)/shard_map/ppermute | solution.py:17
  292.2 20.9 %collective-permute-start.8 = (f32[1,8,3072]{2,1,0:T(8,128)S(1)}, f32[1,8,3072]{2,1,0:T(8,128)S(1)}, u32[]{:S(2)}, u32[]{:S(2)}) collective-permute-start(f32[1,8,3072]{2,1,0:T(8,128)S(1)} %copy.28), channel_id=1, source_target_pairs={{0,4},{4,8},{8,12},{12,16},{16,20},{20,24},{24,28},{1,5},{5,9},{9,... | collective-permute-start | bytes 294920 | tf_op jit(solution)/shard_map/ppermute | solution.py:16
  367.0 43.2 %collective-permute-start.10 = (f32[1,1536,8]{1,2,0:T(8,128)S(1)}, f32[1,1536,8]{1,2,0:T(8,128)S(1)}, u32[]{:S(2)}, u32[]{:S(2)}) collective-permute-start(f32[1,1536,8]{1,2,0:T(8,128)S(1)} %get-tuple-element.27), channel_id=1, source_target_pairs={{0,1},{1,2},{2,3},{4,5},{5,6},{6,7},{8,9},{9,10},{10,11},{12,13},{... | collective-permute-start | bytes 147464 | tf_op jit(solution)/shard_map/ppermute | solution.py:16
  408.8 3.1 collective-permute-start.11
where the time goes:
time: 549 us; the launch traced here: 547 us
  other arithmetic  308 us (56%)
  local copies, waits for them, and re-layouts  149 us (27%)
  blocking collectives  44.6 us (8%)
  starting transfers between devices  35 us (6%)
  waiting for transfers between devices  7.45 us (1%)
    add x3, other arithmetic, filter_dim(): return outer + inner + part(2 * step, 2 * step) * 0.375  152 us
    reduce_sum x3, other arithmetic, record(): square = jnp.sum(plane * plane, axis=(1, 2))  152 us
    unnamed x5, local copies, waits for them, and re-layouts  93.2 us
    psum x1, blocking collectives, record(): square = lax.psum(square, ('rows', 'cols'))  44.6 us
    ppermute x6, starting transfers between devices, padded_2(): before = lax.ppermute(last, axis, up)  27.2 us
    slice x8, local copies, waits for them, and re-layouts, padded_2(): last = lax.slice_in_dim(array, length - width, length, axis=dim)  19.7 us
    rev x6, local copies, waits for them, and re-layouts, mirror_edges(): jnp.flip(lax.slice_in_dim(padded, length - 2 * width - 1, length - width...  18.8 us
  transfers between devices with their start and end apart: 12, of which 3 were waited for; matrix products, arithmetic and copies ran while one was open for 17% of the time, Pallas kernels for 0%

commit v1 on v0

--- a/solution.py
+++ b/solution.py
@@ -55,7 +55,7 @@
 
     def record(plane):
         square = jnp.sum(plane * plane, axis=(1, 2))
-        square = lax.psum(square, ("rows", "cols"))
+        square = jnp.sum(lax.all_gather(square, ("rows", "cols")), axis=0)
         sigma_rows.append(jnp.sqrt(square / pixels + 1e-06))
 
     current = cube

time: 549 us -> 560 us (1.020)
  local copies, waits for them, and re-layouts: 149 us -> 161 us
    psum x1 -> x0, blocking collectives: 44.6 us -> none  [record(): square = lax.psum(square, ('rows', 'cols'))]
    unnamed x0 -> x1, blocking collectives: none -> 43.3 us
    rev x6, local copies, waits for them, and re-layouts: 5.64 us -> 26 us  [mirror_edges(): jnp.flip(lax.slice_in_dim(padded, width + 1, 2 * width + 1, axis=dim), dim)]
    rev x6, local copies, waits for them, and re-layouts: 18.8 us -> 12.3 us  [mirror_edges(): jnp.flip(lax.slice_in_dim(padded, length - 2 * width - 1, length - width...]
    unnamed x5 -> x11, local copies, waits for them, and re-layouts: 93.2 us -> 95.5 us
  transfers between devices with their start and end apart: 12 -> 12, of which waited for: 3 -> 4; matrix products, arithmetic and copies ran while one was open for 17% -> 15% of each run, Pallas kernels for 0% -> 0%
where the time goes in v1:
time: 560 us; the launch traced here: 556 us
  other arithmetic  309 us (55%)
  local copies, waits for them, and re-layouts  161 us (29%)
  blocking collectives  43.3 us (8%)
  starting transfers between devices  33.1 us (6%)
  waiting for transfers between devices  6.71 us (1%)
    reduce_sum x3, other arithmetic, record(): square = jnp.sum(plane * plane, axis=(1, 2))  152 us
    add x3, other arithmetic, filter_dim(): return outer + inner + part(2 * step, 2 * step) * 0.375  152 us
    unnamed x11, local copies, waits for them, and re-layouts  95.5 us
    unnamed x1, blocking collectives  43.3 us
    rev x6, local copies, waits for them, and re-layouts, mirror_edges(): jnp.flip(lax.slice_in_dim(padded, width + 1, 2 * width + 1, axis=dim), dim)  26 us
    ppermute x6, starting transfers between devices, padded_2(): before = lax.ppermute(last, axis, up)  25 us
    slice x8, local copies, waits for them, and re-layouts, padded_2(): last = lax.slice_in_dim(array, length - width, length, axis=dim)  18.3 us
    rev x6, local copies, waits for them, and re-layouts, mirror_edges(): jnp.flip(lax.slice_in_dim(padded, length - 2 * width - 1, length - width...  12.3 us
  transfers between devices with their start and end apart: 12, of which 4 were waited for; matrix products, arithmetic and copies ran while one was open for 15% of the time, Pallas kernels for 0%

profile of v1, /device:TPU:0, one launch (start us, length us, event | category | flops | bytes accessed | tf_op | source)
XLA Modules:
  0.0 556.5 jit_solution(13084219282917614988)
XLA Ops:
  1.7 4.9 collective-permute-start
  7.9 18.6 %copy.23 = f32[1,1536,3072]{1,2,0:T(8,128)} copy(f32[1,1536,3072]{2,1,0:T(8,128)} %param.1) | data formatting | bytes 37748736 | tf_op args[0]
  28.8 50.3 %fusion.34 = f32[1,1536,3072]{1,2,0:T(8,128)} fusion(f32[1,1536,3072]{1,2,0:T(8,128)} %copy.23, f32[1,2,3072]{1,2,0:T(8,128)S(1)} %copy.21, f32[1,2,3072]{1,2,0:T(8,128)S(1)} %copy.18), kind=kLoop, calls=%fused_computation.58 | loop fusion | flops 51904512 | bytes 37797888 | tf_op jit(solution)/shard_map/add | solution.py:30
  83.5 3.0 collective-permute-done.3
  86.5 50.7 %multiply_reduce_fusion.2 = (f32[]{:T(128)}, f32[1,1536,3072]{1,2,0:T(8,128)}, f32[1,1536,3072]{1,2,0:T(8,128)}) fusion(f32[1,1536,3072]{1,2,0:T(8,128)} %copy.23, f32[1,1536,3072]{1,2,0:T(8,128)} %fusion.34, f32[1,1536,2]{1,2,0:T(2,128)S(1)} %broadcast_select_fusion.10, f32[1,1536,2]{1,2,0:T(2,128)S(1)} %broadcast_select_fusion.11), kind=kLoop, calls=%fused_computation.86 | loop fusion | flops 66060288 | bytes 75522048 | tf_op jit(solution)/shard_map/reduce_sum | solution.py:57
  137.2 6.1 %fusion.54 = (f32[1,4,3072]{1,2,0:T(8,128)S(1)}, f32[1,4,3072]{1,2,0:T(8,128)}, f32[1,4,3072]{1,2,0:T(8,128)S(1)}, f32[1,4,3072]{1,2,0:T(8,128)}) fusion(f32[1,1536,3072]{1,2,0:T(8,128)} %get-tuple-element.20), kind=kLoop, calls=%fused_computation.103 | loop fusion | bytes 393216 | tf_op jit(solution)/shard_map/slice | solution.py:14
  143.8 4.5 collective-permute-start.4
  148.3 11.2 %rev.46 = f32[1,4,3072]{1,2,0:T(8,128)S(1)} reverse(f32[1,4,3072]{1,2,0:T(8,128)} %get-tuple-element.42), dimensions={1} | reverse | bytes 98304 | tf_op jit(solution)/shard_map/jit(_flip)/rev | solution.py:35
  159.5 1.9 copy.26
  162.9 8.7 %rev.47 = f32[1,4,3072]{1,2,0:T(8,128)} reverse(f32[1,4,3072]{1,2,0:T(8,128)S(1)} %get-tuple-element.41), dimensions={1} | reverse | bytes 98304 | tf_op jit(solution)/shard_map/jit(_flip)/rev | solution.py:36
  171.6 1.7 copy.25
  174.1 50.7 %fusion.28 = f32[1,1536,3072]{1,2,0:T(8,128)} fusion(f32[1,1536,3072]{1,2,0:T(8,128)} %get-tuple-element.20, f32[1,4,3072]{1,2,0:T(8,128)S(1)} %broadcast_select_fusion.2, f32[1,4,3072]{1,2,0:T(8,128)S(1)} %broadcast_select_fusion.3), kind=kLoop, calls=%fused_computation.52 | loop fusion | flops 51904512 | bytes 37847040 | tf_op jit(solution)/shard_map/add | solution.py:30
  225.7 4.1 collective-permute-start.6
  233.2 50.9 %multiply_reduce_fusion.1 = (f32[]{:T(128)}, f32[1,1536,3072]{1,2,0:T(8,128)}, f32[1,1536,3072]{1,2,0:T(8,128)}) fusion(f32[1,1536,3072]{1,2,0:T(8,128)} %get-tuple-element.20, f32[1,1536,3072]{1,2,0:T(8,128)} %fusion.28, f32[1,1536,4]{1,2,0:T(4,128)S(1)} %broadcast_select_fusion.8, f32[1,1536,4]{1,2,0:T(4,128)S(1)} %broadcast_select_fusion.9), kind=kLoop, calls=%fused_computation.85 | loop fusion | flops 66060288 | bytes 75546624 | tf_op jit(solution)/shard_map/reduce_sum | solution.py:57
  284.1 6.1 %fusion.52 = (f32[1,8,3072]{1,2,0:T(8,128)}, f32[1,8,3072]{1,2,0:T(8,128)S(1)}, f32[1,8,3072]{1,2,0:T(8,128)S(1)}, f32[1,8,3072]{1,2,0:T(8,128)}) fusion(f32[1,1536,3072]{1,2,0:T(8,128)} %get-tuple-element.23), kind=kLoop, calls=%fused_computation.101 | loop fusion | bytes 786432 | tf_op jit(solution)/shard_map/slice | solution.py:14
  290.2 1.8 copy.28
  292.0 6.4 %collective-permute-start.8 = (f32[1,8,3072]{2,1,0:T(8,128)S(1)}, f32[1,8,3072]{2,1,0:T(8,128)S(1)}, u32[]{:S(2)}, u32[]{:S(2)}) collective-permute-start(f32[1,8,3072]{2,1,0:T(8,128)S(1)} %copy.28), channel_id=1, source_target_pairs={{0,4},{4,8},{8,12},{12,16},{16,20},{20,24},{24,28},{1,5},{5,9},{9,... | collective-permute-start | bytes 294920 | tf_op jit(solution)/shard_map/ppermute | solution.py:16
  298.4 13.4 %rev.50 = f32[1,8,3072]{1,2,0:T(8,128)} reverse(f32[1,8,3072]{1,2,0:T(8,128)} %get-tuple-element.34), dimensions={1} | reverse | bytes 196608 | tf_op jit(solution)/shard_map/jit(_flip)/rev | solution.py:35
  313.8 2.1 rev.51
  315.9 1.6 copy.29
  317.5 1.6 broadcast_select_fusion.1
  319.5 1.6 copy.31
  321.1 1.6 broadcast_select_fusion
  322.7 50.7 %fusion.22 = f32[1,1536,3072]{1,2,0:T(8,128)} fusion(f32[1,1536,3072]{1,2,0:T(8,128)} %get-tuple-element.23, f32[1,8,3072]{1,2,0:T(8,128)S(1)} %broadcast_select_fusion, f32[1,8,3072]{1,2,0:T(8,128)S(1)} %broadcast_select_fusion.1), kind=kLoop, calls=%fused_computation.46 | loop fusion | flops 51904512 | bytes 37945344 | tf_op jit(solution)/shard_map/add | solution.py:30
  374.4 3.6 collective-permute-start.10
  378.1 18.6 %copy.32 = f32[1,1536,3072]{2,1,0:T(8,128)} copy(f32[1,1536,3072]{1,2,0:T(8,128)} %get-tuple-element.19) | data formatting | bytes 37748736
  399.9 1.9 collective-permute-done.11
  401.8 50.2 %multiply_reduce_fusion = (f32[]{:T(128)}, f32[1,1536,3072]{1,2,0:T(8,128)}, f32[1,1536,3072]{1,2,0:T(8,128)}) fusion(f32[1,1536,3072]{1,2,0:T(8,128)} %get-tuple-element.23, f32[1,1536,3072]{1,2,0:T(8,128)} %fusion.22, f32[1,1536,8]{1,2,0:T(8,128)S(1)} %broadcast_select_fusion.4, f32[1,1536,8]{1,2,0:T(8,128)S(1)} %broadcast_select_fusion.5), kind=kLoop, calls=%fused_computation.84 | loop fusion | flops 66060288 | bytes 75595776 | tf_op jit(solution)/shard_map/reduce_sum | solution.py:57
  452.8 18.6 %copy.33 = f32[1,1536,3072]{2,1,0:T(8,128)} copy(f32[1,1536,3072]{1,2,0:T(8,128)} %get-tuple-element.22) | data formatting | bytes 37748736
  471.4 43.3 %all-reduce.3 = (f32[32]{0:T(128)S(1)}, f32[32]{0:T(128)S(1)}, f32[32]{0:T(128)S(1)}) all-reduce(f32[32]{0:T(128)S(1)} %dynamic-update-slice.2, f32[32]{0:T(128)S(1)} %dynamic-update-slice.1, f32[32]{0:T(128)S(1)} %dynamic-update-slice), channel_id=1, replica_groups=mesh['rows'=8,'cols'=4] {'rows','cols'}, use_global_device_ids=true, to_apply=%add.2 | all-reduce | flops 96 | bytes 768
  518.6 18.6 %copy.34 = f32[1,1536,3072]{2,1,0:T(8,128)} copy(f32[1,1536,3072]{1,2,0:T(8,128)} %get-tuple-element.25) | data formatting | bytes 37748736
  537.2 18.6 %copy.35 = f32[1,1536,3072]{2,1,0:T(8,128)} copy(f32[1,1536,3072]{1,2,0:T(8,128)} %get-tuple-element.26) | data formatting | bytes 37748736
  (54 shorter events, 25.6 us)
Async XLA Ops:
  1.7 26.0 %collective-permute-start = (f32[1,2,3072]{2,1,0:T(2,128)S(1)}, f32[1,2,3072]{2,1,0:T(2,128)S(1)}, u32[]{:S(2)}, u32[]{:S(2)}) collective-permute-start(f32[1,2,3072]{2,1,0:T(2,128)S(1)} %get-tuple-element.47), channel_id=1, source_target_pairs={{0,4},{4,8},{8,12},{12,16},{16,20},{20,24},{24,28},{1,5},{5,9},{9,... | collective-permute-start | bytes 73736 | tf_op jit(solution)/shard_map/ppermute | solution.py:16
  6.6 21.7 %collective-permute-start.1 = (f32[1,2,3072]{2,1,0:T(2,128)S(1)}, f32[1,2,3072]{2,1,0:T(2,128)S(1)}, u32[]{:S(2)}, u32[]{:S(2)}) collective-permute-start(f32[1,2,3072]{2,1,0:T(2,128)S(1)} %get-tuple-element.48), channel_id=1, source_target_pairs={{4,0},{8,4},{12,8},{16,12},{20,16},{24,20},{28,24},{5,1},{9,5},{13... | collective-permute-start | bytes 73736 | tf_op jit(solution)/shard_map/ppermute | solution.py:17
  80.0 3.4 collective-permute-start.2
  81.8 4.7 collective-permute-start.3
  143.8 27.9 %collective-permute-start.4 = (f32[1,4,3072]{2,1,0:T(4,128)S(1)}, f32[1,4,3072]{2,1,0:T(4,128)S(1)}, u32[]{:S(2)}, u32[]{:S(2)}) collective-permute-start(f32[1,4,3072]{2,1,0:T(4,128)S(1)} %copy.24), channel_id=1, source_target_pairs={{0,4},{4,8},{8,12},{12,16},{16,20},{20,24},{24,28},{1,5},{5,9},{9,... | collective-permute-start | bytes 147464 | tf_op jit(solution)/shard_map/ppermute | solution.py:16
  161.4 12.0 %collective-permute-start.5 = (f32[1,4,3072]{2,1,0:T(4,128)S(1)}, f32[1,4,3072]{2,1,0:T(4,128)S(1)}, u32[]{:S(2)}, u32[]{:S(2)}) collective-permute-start(f32[1,4,3072]{2,1,0:T(4,128)S(1)} %copy.26), channel_id=1, source_target_pairs={{4,0},{8,4},{12,8},{16,12},{20,16},{24,20},{28,24},{5,1},{9,5},{13... | collective-permute-start | bytes 147464 | tf_op jit(solution)/shard_map/ppermute | solution.py:17
  225.7 6.0 %collective-permute-start.6 = (f32[1,1536,4]{1,2,0:T(4,128)S(1)}, f32[1,1536,4]{1,2,0:T(4,128)S(1)}, u32[]{:S(2)}, u32[]{:S(2)}) collective-permute-start(f32[1,1536,4]{1,2,0:T(4,128)S(1)} %get-tuple-element.35), channel_id=1, source_target_pairs={{0,1},{1,2},{2,3},{4,5},{5,6},{6,7},{8,9},{9,10},{10,11},{12,13},{... | collective-permute-start | bytes 73736 | tf_op jit(solution)/shard_map/ppermute | solution.py:16
  230.1 3.1 collective-permute-start.7
  292.0 23.9 %collective-permute-start.8 = (f32[1,8,3072]{2,1,0:T(8,128)S(1)}, f32[1,8,3072]{2,1,0:T(8,128)S(1)}, u32[]{:S(2)}, u32[]{:S(2)}) collective-permute-start(f32[1,8,3072]{2,1,0:T(8,128)S(1)} %copy.28), channel_id=1, source_target_pairs={{0,4},{4,8},{8,12},{12,16},{16,20},{20,24},{24,28},{1,5},{5,9},{9,... | collective-permute-start | bytes 294920 | tf_op jit(solution)/shard_map/ppermute | solution.py:16
  312.3 7.2 %collective-permute-start.9 = (f32[1,8,3072]{2,1,0:T(8,128)S(1)}, f32[1,8,3072]{2,1,0:T(8,128)S(1)}, u32[]{:S(2)}, u32[]{:S(2)}) collective-permute-start(f32[1,8,3072]{2,1,0:T(8,128)S(1)} %copy.30), channel_id=1, source_target_pairs={{4,0},{8,4},{12,8},{16,12},{20,16},{24,20},{28,24},{5,1},{9,5},{13... | collective-permute-start | bytes 294920 | tf_op jit(solution)/shard_map/ppermute | solution.py:17
  374.4 25.5 %collective-permute-start.10 = (f32[1,1536,8]{1,2,0:T(8,128)S(1)}, f32[1,1536,8]{1,2,0:T(8,128)S(1)}, u32[]{:S(2)}, u32[]{:S(2)}) collective-permute-start(f32[1,1536,8]{1,2,0:T(8,128)S(1)} %get-tuple-element.27), channel_id=1, source_target_pairs={{0,1},{1,2},{2,3},{4,5},{5,6},{6,7},{8,9},{9,10},{10,11},{12,13},{... | collective-permute-start | bytes 147464 | tf_op jit(solution)/shard_map/ppermute | solution.py:16
  398.4 3.4 collective-permute-start.11
